TPU v7x, 512 devices: a whole 4x4x16 slice. The times are simulated.
512 devices in a mesh: term: 8 (over y, core), doc: 16 (over z), enc: 4 (over x).
Axes of the slice: x: 4, y: 4, z: 16, core: 2. Of those that a mesh axis runs over, the one named last changes fastest.
Arguments:
- query_weights: bfloat16 [1024, 30720], P('enc', ('term', 'doc')), may hold values from 0.049804688 to 2
- tile_terms: int32 [30720], P(('term', 'doc')), may hold values from 0 to 59
- tile_blocks: int32 [30720], P(('term', 'doc')), may hold values from 0 to 15
- tile_counts: int32 [128], P(('term', 'doc')), may hold values from 60 to 240, as said below
- impacts: bfloat16 [30720, 64, 128], P(('term', 'doc')), may hold values from -0.015625 to 0.015625
Outputs:
- scores: float32 [2048, 1024], P('doc', 'enc')
Inputs may be any that keep to these rules, and one draw needn't show every extreme that they name: Slots at positions tile_counts or later of a device's list are padding and contribute nothing; some device has all 240 slots live.
All inputs are finite; a program needn't handle non-finite values.
Results may differ from a plain program's by a relative error of at most 0.0003.
Values may be sent and summed in bfloat16 or wider, within the bound.
No kernel may reach another device: no remote copies, remote signals or barrier semaphores. Data moves between devices by JAX's collectives and lax.ppermute only.
A program may use at most 64 MiB of HBM per device.

v0:
```python
import jax
import jax.numpy as jnp
from jax import lax
from jax.sharding import PartitionSpec as P


def block_size(tiles):
    largest = 1
    for divisor in range(1, 65):
        if tiles % divisor == 0:
            largest = divisor
    return largest


def per_device(query_weights, tile_terms, tile_blocks, tile_counts, impacts):
    range_rows = lax.all_gather(query_weights, "doc", axis=1, tiled=True)
    queries = range_rows.shape[0]
    tiles, term_block, doc_block = impacts.shape
    owners = lax.axis_size("doc")
    grouped = range_rows.reshape(queries, range_rows.shape[1] // term_block, term_block)
    step = block_size(tiles)
    live = jnp.arange(tiles, dtype=jnp.int32) < tile_counts[0]
    owner_ids = jnp.arange(owners, dtype=jnp.int32)

    def accumulate(total, number):
        start = number * step
        term_now = lax.dynamic_slice_in_dim(tile_terms, start, step)
        owner_now = lax.dynamic_slice_in_dim(tile_blocks, start, step)
        keep_now = lax.dynamic_slice_in_dim(live, start, step)
        tile_now = lax.dynamic_slice_in_dim(impacts, start, step)
        picked = jnp.take(grouped, term_now, axis=1)
        product = jnp.einsum("qnk,nkd->ndq", picked, tile_now, preferred_element_type=jnp.float32)
        select = ((owner_now[:, None] == owner_ids[None, :]) & keep_now[:, None]).astype(
            jnp.float32
        )
        added = jnp.einsum("ndq,nb->bdq", product, select, precision=lax.Precision.HIGHEST)
        return (total + added, None)

    start_total = jnp.zeros((owners, doc_block, queries), jnp.float32)
    total, unused = lax.scan(accumulate, start_total, jnp.arange(tiles // step, dtype=jnp.int32))
    partial_value = total.reshape(owners * doc_block, queries)
    mine = lax.psum_scatter(partial_value, "doc", scatter_dimension=0, tiled=True)
    scores = lax.psum(mine, "term")
    return scores


def solution(mesh):
    return jax.shard_map(
        per_device,
        mesh=mesh,
        in_specs=(
            P("enc", ("term", "doc")),
            P(("term", "doc")),
            P(("term", "doc")),
            P(("term", "doc")),
            P(("term", "doc"), None, None),
        ),
        out_specs=P("doc", "enc"),
        check_vma=False,
    )
```

profile of v0, /device:TPU:2, one launch (start us, length us, event | category | flops | bytes accessed | tf_op | source)
XLA Modules:
  0.0 312.8 jit_solution(1491762189442942286)
XLA Ops:
  6.5 0.7 all-gather.2.cloned.1.call-update
  8.0 78.3 %all-gather.2.cloned.1.call-done = bf16[256,3840]{0,1:T(8,128)(2,1)} async-done(((bf16[256,240]{0,1:T(8,128)(2,1)}), bf16[256,3840]{0,1:T(8,128)(2,1)}) %all-gather.2.cloned.1.call-update) | async-done | bytes 1966096 | tf_op jit(solution)/shard_map/all_gather | solution.py:16
  86.2 67.8 %while.11 = (s32[]{:T(128)}, f32[16,128,256]{2,0,1:T(8,128)}, s32[4]{0:T(128)S(1)}, s32[240]{0:T(256)}, pred[240]{0:T(512)(128)(4,1)S(1)}, /*index=5*/bf16[240,6...) while((s32[]{:T(128)}, f32[16,128,256]{2,0,1:T(8,128)}, ...), condition=%wide.region_1.2_spmd.clone, body=%wide.region_0.1_spmd.clone.sunk | while | flops 631180544 | bytes 43587780 | solution.py:40
  86.2 0.6 dynamic_slice.30
  87.6 0.8 dynamic_slice.31
  88.3 0.8 compare_and_fusion.2
  89.1 2.2 gather_fusion
  91.3 2.6 fusion.28
  93.9 7.9 %select_add_fusion.2 = f32[16,128,256]{2,0,1:T(8,128)S(1)} fusion(f32[16,128,256]{2,0,1:T(8,128)S(1)} %copy-done, f32[60,128,256]{2,1,0:T(8,128)S(1)} %fusion.28, pred[]{:T(512)S(6)} %compare.3, s32[60]{0:T(128)S(1)} %dynamic_slice.31, pred[60]{0:T(512)(128)(4,1)S(1)} %dynamic_slice.32), kind=kOutput, calls=%fused_computation.4.clone.1 | convolution fusion | flops 378537856 | bytes 12058925 | tf_op jit(solution)/shard_map/while/body/eval_jaxpr/ndq,nb->bdq/dot_general | solution.py:36
  101.9 1.3 copy-done.1
  104.5 0.8 dynamic_slice.31
  105.2 0.8 compare_and_fusion.2
  106.0 2.2 gather_fusion
  108.3 2.6 fusion.28
  110.9 7.9 %select_add_fusion.2 = f32[16,128,256]{2,0,1:T(8,128)S(1)} fusion(f32[16,128,256]{2,0,1:T(8,128)S(1)} %copy-done, f32[60,128,256]{2,1,0:T(8,128)S(1)} %fusion.28, pred[]{:T(512)S(6)} %compare.3, s32[60]{0:T(128)S(1)} %dynamic_slice.31, pred[60]{0:T(512)(128)(4,1)S(1)} %dynamic_slice.32), kind=kOutput, calls=%fused_computation.4.clone.1 | convolution fusion | flops 378537856 | bytes 12058925 | tf_op jit(solution)/shard_map/while/body/eval_jaxpr/ndq,nb->bdq/dot_general | solution.py:36
  118.8 1.3 copy-done.1
  121.4 0.8 dynamic_slice.31
  122.2 0.8 compare_and_fusion.2
  122.9 2.2 gather_fusion
  125.2 2.6 fusion.28
  127.8 7.9 %select_add_fusion.2 = f32[16,128,256]{2,0,1:T(8,128)S(1)} fusion(f32[16,128,256]{2,0,1:T(8,128)S(1)} %copy-done, f32[60,128,256]{2,1,0:T(8,128)S(1)} %fusion.28, pred[]{:T(512)S(6)} %compare.3, s32[60]{0:T(128)S(1)} %dynamic_slice.31, pred[60]{0:T(512)(128)(4,1)S(1)} %dynamic_slice.32), kind=kOutput, calls=%fused_computation.4.clone.1 | convolution fusion | flops 378537856 | bytes 12058925 | tf_op jit(solution)/shard_map/while/body/eval_jaxpr/ndq,nb->bdq/dot_general | solution.py:36
  135.7 1.3 copy-done.1
  138.4 0.8 dynamic_slice.31
  139.1 0.8 compare_and_fusion.2
  139.9 2.2 gather_fusion
  142.1 2.6 fusion.28
  144.8 7.9 %select_add_fusion.2 = f32[16,128,256]{2,0,1:T(8,128)S(1)} fusion(f32[16,128,256]{2,0,1:T(8,128)S(1)} %copy-done, f32[60,128,256]{2,1,0:T(8,128)S(1)} %fusion.28, pred[]{:T(512)S(6)} %compare.3, s32[60]{0:T(128)S(1)} %dynamic_slice.31, pred[60]{0:T(512)(128)(4,1)S(1)} %dynamic_slice.32), kind=kOutput, calls=%fused_computation.4.clone.1 | convolution fusion | flops 378537856 | bytes 12058925 | tf_op jit(solution)/shard_map/while/body/eval_jaxpr/ndq,nb->bdq/dot_general | solution.py:36
  152.7 1.3 copy-done.1
  154.0 4.1 %copy.8 = f32[16,128,256]{2,1,0:T(8,128)} copy(f32[16,128,256]{2,0,1:T(8,128)} %get-tuple-element.52) | data formatting | bytes 4194304 | tf_op jit(solution)/shard_map/while | solution.py:40
  158.2 71.0 %reduce-scatter.2.cloned.1.call-done = f32[128,256]{1,0:T(8,128)} async-done(((f32[2048,256]{1,0:T(8,128)}), f32[128,256]{1,0:T(8,128)}) %reduce-scatter.2.cloned.1.call-update) | async-done | bytes 131088 | tf_op jit(solution)/shard_map/reduce_scatter | solution.py:42
  229.3 75.4 %all-reduce.2.cloned.1.call-done = f32[128,256]{1,0:T(8,128)} async-done(((f32[128,256]{1,0:T(8,128)}), f32[128,256]{1,0:T(8,128)}) %all-reduce.2.cloned.1.call-update) | async-done | bytes 131088 | tf_op jit(solution)/shard_map/psum | solution.py:43
  304.7 1.6 copy.24
  (31 shorter events, 2.3 us)
Async XLA Ops:
  6.5 79.7 %all-gather.2.cloned.1.call-start = ((), (), s32[]{:S(2)}) async-start(), calls=%async_computation.1 | async-start | bytes 2088960 | tf_op jit(solution)/shard_map/all_gather | solution.py:16
  7.3 222.0 %reduce-scatter.2.cloned.1.call-start = ((), (), s32[]{:S(2)}) async-start(), calls=%async_computation.2 | async-start | bytes 2228224 | tf_op jit(solution)/shard_map/reduce_scatter | solution.py:42
  91.3 2.6 copy-start
  101.8 1.3 copy-start.1
  108.2 2.6 copy-start
  118.8 1.3 copy-start.1
  125.2 2.6 copy-start
  135.7 1.3 copy-start.1
  142.1 2.6 copy-start
  152.7 1.3 copy-start.1
  158.2 146.6 %all-reduce.2.cloned.1.call-start = ((), (), s32[]{:S(2)}) async-start(), calls=%async_computation.3 | async-start | bytes 262144 | tf_op jit(solution)/shard_map/psum | solution.py:43
Sparse Core Ops, SparseCore 0:
  9.4 76.7 all-gather.1
  158.3 70.9 reduce-scatter.1
  231.6 73.0 all-reduce.1
where the time goes:
time: 313 us
  waiting for transfers between devices  225 us (72%)
  matrix products  42 us (13%)
  local copies, waits for them, and re-layouts  25.7 us (8%)
  between operations  13.8 us (4%)
    all_gather x1, waiting for transfers between devices, per_device(): range_rows = lax.all_gather(query_weights, 'doc', axis=1, tiled=True)  78.3 us
    psum x1, waiting for transfers between devices, per_device(): scores = lax.psum(mine, 'term')  75.4 us
    reduce_scatter x1, waiting for transfers between devices, per_device(): lax.psum_scatter(partial_value, 'doc', scatter_dimension=0, tiled=True)  71 us
    dot_general x4, matrix products, accumulate(): jnp.einsum('ndq,nb->bdq', product, select, precision=lax.Precision.HIGHEST)  31.6 us
    dot_general x4, matrix products, accumulate(): jnp.einsum('qnk,nkd->ndq', picked, tile_now, preferred_element_type=jnp.f...  10.5 us
    gather x4, local copies, waits for them, and re-layouts, accumulate(): picked = jnp.take(grouped, term_now, axis=1)  8.92 us
  transfers between devices with their start and end apart: 3, of which 3 were waited for; matrix products, arithmetic and copies ran while one was open for 0% of the time, Pallas kernels for 0%

commit v1 on v0

--- a/solution.py
+++ b/solution.py
@@ -2,6 +2,12 @@
 import jax.numpy as jnp
 from jax import lax
 from jax.sharding import PartitionSpec as P
+
+
+def laid_out(pieces, dim):
+    pieces = jnp.moveaxis(pieces, 0, dim)
+    shape = pieces.shape
+    return pieces.reshape(*shape[:dim], shape[dim] * shape[dim + 1], *shape[dim + 2 :])
 
 
 def block_size(tiles):
@@ -13,7 +19,19 @@
 
 
 def per_device(query_weights, tile_terms, tile_blocks, tile_counts, impacts):
-    range_rows = lax.all_gather(query_weights, "doc", axis=1, tiled=True)
+    size = lax.axis_size("doc")
+    pairs = [(i, (i + 1) % size) for i in range(size)]
+    back = [(b, a) for a, b in pairs]
+    lower, upper = ([], [])
+    for turn in range(size - 1):
+        if turn % 2 == 0:
+            lower.append(lax.ppermute(lower[-1] if lower else query_weights, "doc", pairs))
+        else:
+            upper.append(lax.ppermute(upper[-1] if upper else query_weights, "doc", back))
+    blocks = jnp.stack([*lower[::-1], query_weights, *upper])
+    shift = lax.axis_index("doc") - len(lower)
+    blocks = blocks[(jnp.arange(size) - shift) % size]
+    range_rows = laid_out(blocks, 1)
     queries = range_rows.shape[0]
     tiles, term_block, doc_block = impacts.shape
     owners = lax.axis_size("doc")

time: 313 us -> 308 us (0.984)
  waiting for transfers between devices: 225 us -> 165 us
  starting transfers between devices: 0.08 us -> 54.6 us
    all_gather x1 -> x0, waiting for transfers between devices: 78.3 us -> none  [per_device(): range_rows = lax.all_gather(query_weights, 'doc', axis=1, tiled=True)]
    ppermute x0 -> x15, starting transfers between devices: none -> 54.6 us  [the longest x7 37.3 us: per_device(): lax.ppermute(upper[-1] if upper else query_weights, 'doc', back)]
    ppermute x0 -> x15, waiting for transfers between devices: none -> 17 us  [the longest x8 16.9 us: per_device(): lax.ppermute(lower[-1] if lower else query_weights, 'doc', pairs)]
  transfers between devices with their start and end apart: 3 -> 17, of which waited for: 3 -> 10; matrix products, arithmetic and copies ran while one was open for 0% -> 1% of each run, Pallas kernels for 0% -> 0%
where the time goes in v1:
time: 308 us; the launch traced here: 307 us
  waiting for transfers between devices  165 us (54%)
  starting transfers between devices  54.6 us (18%)
  matrix products  42 us (14%)
  local copies, waits for them, and re-layouts  27.7 us (9%)
  between operations  14.4 us (5%)
    psum x1, waiting for transfers between devices, per_device(): scores = lax.psum(mine, 'term')  75.4 us
    reduce_scatter x1, waiting for transfers between devices, per_device(): lax.psum_scatter(partial_value, 'doc', scatter_dimension=0, tiled=True)  72.6 us
    ppermute x7, starting transfers between devices, per_device(): lax.ppermute(upper[-1] if upper else query_weights, 'doc', back)  37.3 us
    dot_general x4, matrix products, accumulate(): jnp.einsum('ndq,nb->bdq', product, select, precision=lax.Precision.HIGHEST)  31.6 us
    ppermute x8, starting transfers between devices, per_device(): lax.ppermute(lower[-1] if lower else query_weights, 'doc', pairs)  17.3 us
    ppermute x8, waiting for transfers between devices, per_device(): lax.ppermute(lower[-1] if lower else query_weights, 'doc', pairs)  16.9 us
    dot_general x4, matrix products, accumulate(): jnp.einsum('qnk,nkd->ndq', picked, tile_now, preferred_element_type=jnp.f...  10.5 us
    gather x4, local copies, waits for them, and re-layouts, accumulate(): picked = jnp.take(grouped, term_now, axis=1)  8.92 us
  transfers between devices with their start and end apart: 17, of which 10 were waited for; matrix products, arithmetic and copies ran while one was open for 1% of the time, Pallas kernels for 0%

profile of v1, /device:TPU:2, one launch (start us, length us, event | category | flops | bytes accessed | tf_op | source)
XLA Modules:
  0.0 306.9 jit_solution(656643797192978390)
XLA Ops:
  6.5 3.9 %collective-permute-start = (bf16[256,240]{0,1:T(8,128)(2,1)}, bf16[256,240]{0,1:T(8,128)(2,1)S(1)}, u32[]{:S(2)}, u32[]{:S(2)}) collective-permute-start(bf16[256,240]{0,1:T(8,128)(2,1)} %param.7), channel_id=1, source_target_pairs={{0,4},{4,8},{8,12},{12,16},{16,20},{20,24},{24,28},{28,32},{32,36}... | collective-permute-start | bytes 368648 | tf_op jit(solution)/shard_map/ppermute | solution.py:28
  10.5 11.1 %collective-permute-done = bf16[256,240]{0,1:T(8,128)(2,1)S(1)} collective-permute-done((bf16[256,240]{0,1:T(8,128)(2,1)}, bf16[256,240]{0,1:T(8,128)(2,1)S(1)}, u32[]{:S(2)}, u32[]{:S(2)}) %collective-permute-start) | collective-permute-done | bytes 122912 | tf_op jit(solution)/shard_map/ppermute | solution.py:28
  21.6 1.9 collective-permute-start.1
  23.5 5.1 %collective-permute-start.8 = (bf16[256,240]{0,1:T(8,128)(2,1)}, bf16[256,240]{0,1:T(8,128)(2,1)S(1)}, u32[]{:S(2)}, u32[]{:S(2)}) collective-permute-start(bf16[256,240]{0,1:T(8,128)(2,1)} %param.7), channel_id=1, source_target_pairs={{4,0},{8,4},{12,8},{16,12},{20,16},{24,20},{28,24},{32,28},{36,32}... | collective-permute-start | bytes 368648 | tf_op jit(solution)/shard_map/ppermute | solution.py:30
  29.6 1.9 collective-permute-start.2
  31.5 5.3 %collective-permute-start.9 = (bf16[256,240]{0,1:T(8,128)(2,1)S(1)}, bf16[256,240]{0,1:T(8,128)(2,1)S(1)}, u32[]{:S(2)}, u32[]{:S(2)}) collective-permute-start(bf16[256,240]{0,1:T(8,128)(2,1)S(1)} %collective-permute-done.8), channel_id=1, source_target_pairs={{4,0},{8,4},{12,8},{16,12},{20,16},{24,20},{28,24},{32,28},{36,32}... | collective-permute-start | bytes 368648 | tf_op jit(solution)/shard_map/ppermute | solution.py:30
  37.5 1.9 collective-permute-start.3
  39.5 5.3 %collective-permute-start.10 = (bf16[256,240]{0,1:T(8,128)(2,1)S(1)}, bf16[256,240]{0,1:T(8,128)(2,1)S(1)}, u32[]{:S(2)}, u32[]{:S(2)}) collective-permute-start(bf16[256,240]{0,1:T(8,128)(2,1)S(1)} %collective-permute-done.9), channel_id=1, source_target_pairs={{4,0},{8,4},{12,8},{16,12},{20,16},{24,20},{28,24},{32,28},{36,32}... | collective-permute-start | bytes 368648 | tf_op jit(solution)/shard_map/ppermute | solution.py:30
  45.5 1.9 collective-permute-start.4
  47.4 5.3 %collective-permute-start.11 = (bf16[256,240]{0,1:T(8,128)(2,1)S(1)}, bf16[256,240]{0,1:T(8,128)(2,1)S(1)}, u32[]{:S(2)}, u32[]{:S(2)}) collective-permute-start(bf16[256,240]{0,1:T(8,128)(2,1)S(1)} %collective-permute-done.10), channel_id=1, source_target_pairs={{4,0},{8,4},{12,8},{16,12},{20,16},{24,20},{28,24},{32,28},{36,32}... | collective-permute-start | bytes 368648 | tf_op jit(solution)/shard_map/ppermute | solution.py:30
  53.5 1.9 collective-permute-start.5
  55.4 5.3 %collective-permute-start.12 = (bf16[256,240]{0,1:T(8,128)(2,1)S(1)}, bf16[256,240]{0,1:T(8,128)(2,1)S(1)}, u32[]{:S(2)}, u32[]{:S(2)}) collective-permute-start(bf16[256,240]{0,1:T(8,128)(2,1)S(1)} %collective-permute-done.11), channel_id=1, source_target_pairs={{4,0},{8,4},{12,8},{16,12},{20,16},{24,20},{28,24},{32,28},{36,32}... | collective-permute-start | bytes 368648 | tf_op jit(solution)/shard_map/ppermute | solution.py:30
  64.8 5.1 %collective-permute-start.13 = (bf16[256,240]{0,1:T(8,128)(2,1)S(1)}, bf16[256,240]{0,1:T(8,128)(2,1)}, u32[]{:S(2)}, u32[]{:S(2)}) collective-permute-start(bf16[256,240]{0,1:T(8,128)(2,1)S(1)} %collective-permute-done.12), channel_id=1, source_target_pairs={{4,0},{8,4},{12,8},{16,12},{20,16},{24,20},{28,24},{32,28},{36,32}... | collective-permute-start | bytes 368648 | tf_op jit(solution)/shard_map/ppermute | solution.py:30
  70.9 1.9 collective-permute-start.7
  72.9 5.7 %collective-permute-start.14 = (bf16[256,240]{0,1:T(8,128)(2,1)}, bf16[256,240]{0,1:T(8,128)(2,1)S(1)}, u32[]{:S(2)}, u32[]{:S(2)}) collective-permute-start(bf16[256,240]{0,1:T(8,128)(2,1)} %collective-permute-done.13), channel_id=1, source_target_pairs={{4,0},{8,4},{12,8},{16,12},{20,16},{24,20},{28,24},{32,28},{36,32}... | collective-permute-start | bytes 368648 | tf_op jit(solution)/shard_map/ppermute | solution.py:30
  82.0 1.9 gather_fusion.1
  84.0 62.3 %while.11 = (s32[]{:T(128)}, f32[16,128,256]{2,0,1:T(8,128)}, s32[4]{0:T(128)S(1)}, s32[240]{0:T(256)S(1)}, pred[240]{0:T(512)(128)(4,1)S(1)}, /*index=5*/bf16[2...) while((s32[]{:T(128)}, f32[16,128,256]{2,0,1:T(8,128)}, ...), condition=%wide.region_1.2_spmd.clone, body=%wide.region_0.1_spmd.clone.sunk | while | flops 631180544 | bytes 43587780 | solution.py:58
  85.5 2.2 gather_fusion
  87.7 2.6 fusion.30
  90.3 7.9 %select_add_fusion.2 = f32[16,128,256]{2,0,1:T(8,128)S(1)} fusion(f32[16,128,256]{2,0,1:T(8,128)S(1)} %copy-done, f32[60,128,256]{2,1,0:T(8,128)S(1)} %fusion.30, pred[]{:T(512)S(6)} %compare.10, s32[60]{0:T(128)S(1)} %dynamic_slice.31, pred[60]{0:T(512)(128)(4,1)S(1)} %dynamic_slice.32), kind=kOutput, calls=%fused_computation.5.clone.1 | convolution fusion | flops 378537856 | bytes 12058925 | tf_op jit(solution)/shard_map/while/body/eval_jaxpr/ndq,nb->bdq/dot_general | solution.py:54
  101.0 2.2 gather_fusion
  103.3 2.6 fusion.30
  105.9 7.9 %select_add_fusion.2 = f32[16,128,256]{2,0,1:T(8,128)S(1)} fusion(f32[16,128,256]{2,0,1:T(8,128)S(1)} %copy-done, f32[60,128,256]{2,1,0:T(8,128)S(1)} %fusion.30, pred[]{:T(512)S(6)} %compare.10, s32[60]{0:T(128)S(1)} %dynamic_slice.31, pred[60]{0:T(512)(128)(4,1)S(1)} %dynamic_slice.32), kind=kOutput, calls=%fused_computation.5.clone.1 | convolution fusion | flops 378537856 | bytes 12058925 | tf_op jit(solution)/shard_map/while/body/eval_jaxpr/ndq,nb->bdq/dot_general | solution.py:54
  116.6 2.2 gather_fusion
  118.9 2.6 fusion.30
  121.5 7.9 %select_add_fusion.2 = f32[16,128,256]{2,0,1:T(8,128)S(1)} fusion(f32[16,128,256]{2,0,1:T(8,128)S(1)} %copy-done, f32[60,128,256]{2,1,0:T(8,128)S(1)} %fusion.30, pred[]{:T(512)S(6)} %compare.10, s32[60]{0:T(128)S(1)} %dynamic_slice.31, pred[60]{0:T(512)(128)(4,1)S(1)} %dynamic_slice.32), kind=kOutput, calls=%fused_computation.5.clone.1 | convolution fusion | flops 378537856 | bytes 12058925 | tf_op jit(solution)/shard_map/while/body/eval_jaxpr/ndq,nb->bdq/dot_general | solution.py:54
  132.2 2.2 gather_fusion
  134.4 2.6 fusion.30
  137.1 7.9 %select_add_fusion.2 = f32[16,128,256]{2,0,1:T(8,128)S(1)} fusion(f32[16,128,256]{2,0,1:T(8,128)S(1)} %copy-done, f32[60,128,256]{2,1,0:T(8,128)S(1)} %fusion.30, pred[]{:T(512)S(6)} %compare.10, s32[60]{0:T(128)S(1)} %dynamic_slice.31, pred[60]{0:T(512)(128)(4,1)S(1)} %dynamic_slice.32), kind=kOutput, calls=%fused_computation.5.clone.1 | convolution fusion | flops 378537856 | bytes 12058925 | tf_op jit(solution)/shard_map/while/body/eval_jaxpr/ndq,nb->bdq/dot_general | solution.py:54
  146.3 4.1 %copy.8 = f32[16,128,256]{2,1,0:T(8,128)} copy(f32[16,128,256]{2,0,1:T(8,128)} %get-tuple-element.52) | data formatting | bytes 4194304 | tf_op jit(solution)/shard_map/while | solution.py:58
  150.5 72.6 %reduce-scatter.2.cloned.1.call-done = f32[128,256]{1,0:T(8,128)} async-done(((f32[2048,256]{1,0:T(8,128)}), f32[128,256]{1,0:T(8,128)}) %reduce-scatter.2.cloned.1.call-update) | async-done | bytes 131088 | tf_op jit(solution)/shard_map/reduce_scatter | solution.py:60
  223.1 75.4 %all-reduce.2.cloned.1.call-done = f32[128,256]{1,0:T(8,128)} async-done(((f32[128,256]{1,0:T(8,128)}), f32[128,256]{1,0:T(8,128)}) %all-reduce.2.cloned.1.call-update) | async-done | bytes 131088 | tf_op jit(solution)/shard_map/psum | solution.py:61
  (85 shorter events, 20.9 us)
Async XLA Ops:
  6.5 74.4 %copy-start.2 = (bf16[256,240]{0,1:T(8,128)(2,1)S(1)}, bf16[256,240]{0,1:T(8,128)(2,1)}, u32[]{:S(2)}) copy-start(bf16[256,240]{0,1:T(8,128)(2,1)} %param.7) | copy-start | bytes 368644
  6.5 216.5 %reduce-scatter.2.cloned.1.call-start = ((), (), s32[]{:S(2)}) async-start(), calls=%async_computation.1 | async-start | bytes 2228224 | tf_op jit(solution)/shard_map/reduce_scatter | solution.py:60
  6.5 15.0 %collective-permute-start = (bf16[256,240]{0,1:T(8,128)(2,1)}, bf16[256,240]{0,1:T(8,128)(2,1)S(1)}, u32[]{:S(2)}, u32[]{:S(2)}) collective-permute-start(bf16[256,240]{0,1:T(8,128)(2,1)} %param.7), channel_id=1, source_target_pairs={{0,4},{4,8},{8,12},{12,16},{16,20},{20,24},{24,28},{28,32},{32,36}... | collective-permute-start | bytes 368648 | tf_op jit(solution)/shard_map/ppermute | solution.py:28
  21.6 8.0 %collective-permute-start.1 = (bf16[256,240]{0,1:T(8,128)(2,1)S(1)}, bf16[256,240]{0,1:T(8,128)(2,1)S(1)}, u32[]{:S(2)}, u32[]{:S(2)}) collective-permute-start(bf16[256,240]{0,1:T(8,128)(2,1)S(1)} %collective-permute-done), channel_id=1, source_target_pairs={{0,4},{4,8},{8,12},{12,16},{16,20},{20,24},{24,28},{28,32},{32,36}... | collective-permute-start | bytes 368648 | tf_op jit(solution)/shard_map/ppermute | solution.py:28
  23.5 8.0 %collective-permute-start.8 = (bf16[256,240]{0,1:T(8,128)(2,1)}, bf16[256,240]{0,1:T(8,128)(2,1)S(1)}, u32[]{:S(2)}, u32[]{:S(2)}) collective-permute-start(bf16[256,240]{0,1:T(8,128)(2,1)} %param.7), channel_id=1, source_target_pairs={{4,0},{8,4},{12,8},{16,12},{20,16},{24,20},{28,24},{32,28},{36,32}... | collective-permute-start | bytes 368648 | tf_op jit(solution)/shard_map/ppermute | solution.py:30
  29.6 8.0 %collective-permute-start.2 = (bf16[256,240]{0,1:T(8,128)(2,1)S(1)}, bf16[256,240]{0,1:T(8,128)(2,1)S(1)}, u32[]{:S(2)}, u32[]{:S(2)}) collective-permute-start(bf16[256,240]{0,1:T(8,128)(2,1)S(1)} %collective-permute-done.1), channel_id=1, source_target_pairs={{0,4},{4,8},{8,12},{12,16},{16,20},{20,24},{24,28},{28,32},{32,36}... | collective-permute-start | bytes 368648 | tf_op jit(solution)/shard_map/ppermute | solution.py:28
  31.5 8.0 %collective-permute-start.9 = (bf16[256,240]{0,1:T(8,128)(2,1)S(1)}, bf16[256,240]{0,1:T(8,128)(2,1)S(1)}, u32[]{:S(2)}, u32[]{:S(2)}) collective-permute-start(bf16[256,240]{0,1:T(8,128)(2,1)S(1)} %collective-permute-done.8), channel_id=1, source_target_pairs={{4,0},{8,4},{12,8},{16,12},{20,16},{24,20},{28,24},{32,28},{36,32}... | collective-permute-start | bytes 368648 | tf_op jit(solution)/shard_map/ppermute | solution.py:30
  37.5 8.0 %collective-permute-start.3 = (bf16[256,240]{0,1:T(8,128)(2,1)S(1)}, bf16[256,240]{0,1:T(8,128)(2,1)S(1)}, u32[]{:S(2)}, u32[]{:S(2)}) collective-permute-start(bf16[256,240]{0,1:T(8,128)(2,1)S(1)} %collective-permute-done.2), channel_id=1, source_target_pairs={{0,4},{4,8},{8,12},{12,16},{16,20},{20,24},{24,28},{28,32},{32,36}... | collective-permute-start | bytes 368648 | tf_op jit(solution)/shard_map/ppermute | solution.py:28
  39.5 8.0 %collective-permute-start.10 = (bf16[256,240]{0,1:T(8,128)(2,1)S(1)}, bf16[256,240]{0,1:T(8,128)(2,1)S(1)}, u32[]{:S(2)}, u32[]{:S(2)}) collective-permute-start(bf16[256,240]{0,1:T(8,128)(2,1)S(1)} %collective-permute-done.9), channel_id=1, source_target_pairs={{4,0},{8,4},{12,8},{16,12},{20,16},{24,20},{28,24},{32,28},{36,32}... | collective-permute-start | bytes 368648 | tf_op jit(solution)/shard_map/ppermute | solution.py:30
  45.5 8.0 %collective-permute-start.4 = (bf16[256,240]{0,1:T(8,128)(2,1)S(1)}, bf16[256,240]{0,1:T(8,128)(2,1)S(1)}, u32[]{:S(2)}, u32[]{:S(2)}) collective-permute-start(bf16[256,240]{0,1:T(8,128)(2,1)S(1)} %collective-permute-done.3), channel_id=1, source_target_pairs={{0,4},{4,8},{8,12},{12,16},{16,20},{20,24},{24,28},{28,32},{32,36}... | collective-permute-start | bytes 368648 | tf_op jit(solution)/shard_map/ppermute | solution.py:28
  47.4 8.0 %collective-permute-start.11 = (bf16[256,240]{0,1:T(8,128)(2,1)S(1)}, bf16[256,240]{0,1:T(8,128)(2,1)S(1)}, u32[]{:S(2)}, u32[]{:S(2)}) collective-permute-start(bf16[256,240]{0,1:T(8,128)(2,1)S(1)} %collective-permute-done.10), channel_id=1, source_target_pairs={{4,0},{8,4},{12,8},{16,12},{20,16},{24,20},{28,24},{32,28},{36,32}... | collective-permute-start | bytes 368648 | tf_op jit(solution)/shard_map/ppermute | solution.py:30
  53.5 8.8 %collective-permute-start.5 = (bf16[256,240]{0,1:T(8,128)(2,1)S(1)}, bf16[256,240]{0,1:T(8,128)(2,1)S(1)}, u32[]{:S(2)}, u32[]{:S(2)}) collective-permute-start(bf16[256,240]{0,1:T(8,128)(2,1)S(1)} %collective-permute-done.4), channel_id=1, source_target_pairs={{0,4},{4,8},{8,12},{12,16},{16,20},{20,24},{24,28},{28,32},{32,36}... | collective-permute-start | bytes 368648 | tf_op jit(solution)/shard_map/ppermute | solution.py:28
  55.4 9.4 %collective-permute-start.12 = (bf16[256,240]{0,1:T(8,128)(2,1)S(1)}, bf16[256,240]{0,1:T(8,128)(2,1)S(1)}, u32[]{:S(2)}, u32[]{:S(2)}) collective-permute-start(bf16[256,240]{0,1:T(8,128)(2,1)S(1)} %collective-permute-done.11), channel_id=1, source_target_pairs={{4,0},{8,4},{12,8},{16,12},{20,16},{24,20},{28,24},{32,28},{36,32}... | collective-permute-start | bytes 368648 | tf_op jit(solution)/shard_map/ppermute | solution.py:30
  62.3 8.7 %collective-permute-start.6 = (bf16[256,240]{0,1:T(8,128)(2,1)S(1)}, bf16[256,240]{0,1:T(8,128)(2,1)S(1)}, u32[]{:S(2)}, u32[]{:S(2)}) collective-permute-start(bf16[256,240]{0,1:T(8,128)(2,1)S(1)} %collective-permute-done.5), channel_id=1, source_target_pairs={{0,4},{4,8},{8,12},{12,16},{16,20},{20,24},{24,28},{28,32},{32,36}... | collective-permute-start | bytes 368648 | tf_op jit(solution)/shard_map/ppermute | solution.py:28
  64.8 8.1 %collective-permute-start.13 = (bf16[256,240]{0,1:T(8,128)(2,1)S(1)}, bf16[256,240]{0,1:T(8,128)(2,1)}, u32[]{:S(2)}, u32[]{:S(2)}) collective-permute-start(bf16[256,240]{0,1:T(8,128)(2,1)S(1)} %collective-permute-done.12), channel_id=1, source_target_pairs={{4,0},{8,4},{12,8},{16,12},{20,16},{24,20},{28,24},{32,28},{36,32}... | collective-permute-start | bytes 368648 | tf_op jit(solution)/shard_map/ppermute | solution.py:30
  70.9 7.7 %copy-start.3 = (bf16[256,240]{0,1:T(8,128)(2,1)}, bf16[256,240]{0,1:T(8,128)(2,1)S(1)}, u32[]{:S(2)}) copy-start(bf16[256,240]{0,1:T(8,128)(2,1)S(1)} %collective-permute-done.6) | copy-start | bytes 368644
  70.9 8.1 %collective-permute-start.7 = (bf16[256,240]{0,1:T(8,128)(2,1)S(1)}, bf16[256,240]{0,1:T(8,128)(2,1)}, u32[]{:S(2)}, u32[]{:S(2)}) collective-permute-start(bf16[256,240]{0,1:T(8,128)(2,1)S(1)} %collective-permute-done.6), channel_id=1, source_target_pairs={{0,4},{4,8},{8,12},{12,16},{16,20},{20,24},{24,28},{28,32},{32,36}... | collective-permute-start | bytes 368648 | tf_op jit(solution)/shard_map/ppermute | solution.py:28
  72.9 9.1 %collective-permute-start.14 = (bf16[256,240]{0,1:T(8,128)(2,1)}, bf16[256,240]{0,1:T(8,128)(2,1)S(1)}, u32[]{:S(2)}, u32[]{:S(2)}) collective-permute-start(bf16[256,240]{0,1:T(8,128)(2,1)} %collective-permute-done.13), channel_id=1, source_target_pairs={{4,0},{8,4},{12,8},{16,12},{20,16},{24,20},{28,24},{32,28},{36,32}... | collective-permute-start | bytes 368648 | tf_op jit(solution)/shard_map/ppermute | solution.py:30
  82.0 2.0 copy-start.4
  82.0 2.0 copy-start.5
  87.7 2.6 copy-start
  98.2 1.3 copy-start.1
  103.3 2.6 copy-start
  113.8 1.3 copy-start.1
  118.9 2.6 copy-start
  129.4 1.3 copy-start.1
  134.4 2.6 copy-start
  145.0 1.3 copy-start.1
  150.4 148.1 %all-reduce.2.cloned.1.call-start = ((), (), s32[]{:S(2)}) async-start(), calls=%async_computation.2 | async-start | bytes 262144 | tf_op jit(solution)/shard_map/psum | solution.py:61
Sparse Core Ops, SparseCore 0:
  150.5 72.4 reduce-scatter.1
  225.3 73.0 all-reduce.1
